TPU v7x, 32 devices: a whole 2x2x4 slice. The times are simulated.
32 devices in a mesh: gx: 4 (over z), gy: 2 (over x), sa: 4 (over y, core).
Axes of the slice: x: 2, y: 2, z: 4, core: 2. Of those that a mesh axis runs over, the one named last changes fastest.
Arguments:
- profile_fields: float32 [32, 4, 32768], P(None, None, ('gx', 'gy', 'sa')), may hold values from -6 to 6
- turbulent_coefficients: float32 [32, 2, 32768], P(None, None, ('gx', 'gy', 'sa')), may hold values from 0.3 to 6
- column_patch_owner: int32 [2, 32768], P(None, ('gx', 'gy', 'sa')), may hold values from 0 to 1023, as said below
- kind_fractions: float32 [6, 32768], P(None, ('gx', 'gy', 'sa')), may hold values from 0.1 to 1
- kind_existing_flags: int32 [5, 32768], P(None, ('gx', 'gy', 'sa')), may hold values 0 or 1
- kind_absorbed_flux: float32 [6, 32768], P(None, ('gx', 'gy', 'sa')), may hold values from -6 to 6
- kind_thermal_links: float32 [6, 32768], P(None, ('gx', 'gy', 'sa')), may hold values from 0.2 to 3
- bottom_kelvin: float32 [6, 32768], P(None, ('gx', 'gy', 'sa')), may hold values from -5 to 5
- drift_speeds: float32 [2, 32768], P(None, ('gx', 'gy', 'sa')), may hold values from -5 to 5
Outputs:
- advanced_profile: float32 [32, 4, 32768], P(None, None, ('gx', 'gy', 'sa'))
- kind_interface_kelvin: float32 [6, 32768], P(None, ('gx', 'gy', 'sa'))
Inputs may be any that keep to these rules, and one draw needn't show every extreme that they name: column_patch_owner[0, i] * 1024 + column_patch_owner[1, i] over all columns i is a permutation of the 32768 cells; row 0 is below 32 and row 1 below 1024. Cell j is held by the device that holds entry j of the cell arrays. The columns of one device have their cells on every device, 1 to 64 of them on each, and exactly 64 on some device.
All inputs are finite; a program needn't handle non-finite values. No bound on the sum of `kind_existing_flags` on one device may be relied on, other than what follows from the above.
Results may differ from a plain program's by a relative error of at most 0.00016.
Values sent between devices are 32-bit elements; how exact they have to be, the bound alone decides.
A program may use at most 64 MiB of HBM per device.

v0:
```python
import functools

import jax
import jax.numpy as jnp
from jax import lax
from jax.experimental import pallas as pl
from jax.experimental.pallas import tpu as pltpu
from jax.sharding import PartitionSpec as P

SWEEPS = 3
AXES = ("gx", "gy", "sa")
LANES = 128
HALF = LANES // 2
GROUP = 32
F32, BF16, I32 = jnp.float32, jnp.bfloat16, jnp.int32
VMEM_GRANT = 60 * 1024 * 1024
FINISH_GRANT = 4 * 1024 * 1024
NT = (((1,), (1,)), ((), ()))
NN = (((1,), (0,)), ((), ()))


def dot(a, b, dims):
    return lax.dot_general(a, b, dims, preferred_element_type=F32)


def halves(x):
    high = x.astype(BF16).astype(F32)
    return high, x - high


def one_hot(mask):
    return jnp.where(mask, 1.0, 0.0).astype(BF16)


def kernel(
    sizes,
    prof_hbm, turb_hbm, owner_hbm, frac_hbm, flag_hbm, flux_hbm, link_hbm, base_hbm, drift_hbm,
    off_all, fac, boundary, kelvin,
    prof, turb, owner_v, frac, flag, flux, link, base, drift,
    rout, lhs, near, code_h, send1, recv1, send2, recv2,
    in_sem, lev_sem, s1, r1, s2, r2,
):
    gx, gy, sa, levels, cols, pieces = sizes
    n = gx * gy * sa
    blocks = cols // LANES
    groups = n // GROUP
    step = levels // pieces
    me = (lax.axis_index("gx") * gy + lax.axis_index("gy")) * sa + lax.axis_index("sa")

    def peer(o):
        q = me + o
        return jnp.where(q >= n, q - n, q)

    def peers(fn):
        if n <= GROUP:
            for o in range(1, n):
                fn(o)
        else:
            def body(o, c):
                fn(o)
                return c
            lax.fori_loop(1, n, body, 0)

    def each_group(fn, init):
        if groups == 1:
            return fn(0, init)
        return lax.fori_loop(0, groups, fn, init)

    loads = [
        pltpu.make_async_copy(a, b, in_sem.at[i])
        for i, (a, b) in enumerate((
            (owner_hbm, owner_v), (frac_hbm, frac), (flag_hbm, flag), (flux_hbm, flux),
            (link_hbm, link), (base_hbm, base), (drift_hbm, drift)))
    ]
    loads[0].start()
    lev_loads = []
    for i in range(pieces):
        rows = pl.ds(i * step, step)
        lev_loads.append((
            pltpu.make_async_copy(turb_hbm.at[rows], turb.at[rows], lev_sem.at[0, i]),
            pltpu.make_async_copy(prof_hbm.at[rows], prof.at[rows], lev_sem.at[1, i])))
        for c in lev_loads[-1]:
            c.start()
    for c in loads[1:]:
        c.start()

    barrier = pltpu.get_barrier_semaphore()
    peers(lambda o: pl.semaphore_signal(
        barrier, inc=1, device_id=peer(o), device_id_type=pl.DeviceIdType.LOGICAL))

    loads[0].wait()
    owner = owner_v[0:1, :]
    local = owner_v[1:2, :]
    onehot_d = lax.broadcasted_iota(I32, (n, cols), 0) == owner
    d01 = one_hot(onehot_d)
    stacked = jnp.concatenate([d01[:, b * LANES:(b + 1) * LANES] for b in range(blocks)], axis=0)
    ti = lax.broadcasted_iota(I32, (LANES, 2 * LANES), 0)
    tj = lax.broadcasted_iota(I32, (LANES, 2 * LANES), 1)
    tri = one_hot((ti < tj) | (tj >= LANES))
    counts = dot(stacked, tri, NN)
    carry = jnp.zeros((n, LANES), F32)
    ranks = []
    for b in range(blocks):
        part = counts[b * n:(b + 1) * n]
        mask = onehot_d[:, b * LANES:(b + 1) * LANES]
        ranks.append(jnp.sum(jnp.where(mask, part[:, :LANES] + carry, 0.0), axis=0, keepdims=True))
        carry = carry + part[:, LANES:]
    rank = jnp.concatenate(ranks, axis=1).astype(I32)
    r01 = one_hot(lax.broadcasted_iota(I32, (HALF, cols), 0) == rank)
    zero = jnp.zeros((HALF, cols), BF16)
    for i in range(2):
        rout[pl.ds(i * LANES, HALF), 0:cols] = r01
        rout[pl.ds(i * LANES, HALF), cols:2 * cols] = zero
        rout[pl.ds(i * LANES + HALF, HALF), 0:cols] = zero
        rout[pl.ds(i * LANES + HALF, HALF), cols:2 * cols] = r01

    def eliminate(row, v, wait):
        above = off = factor = None
        for k in range(levels):
            if wait and k % step == 0:
                for c in lev_loads[k // step]:
                    c.wait()
            below = jnp.broadcast_to(turb[k, row:row + 1, :], (2, cols))
            x = prof[k, v:v + 2, :]
            if k == 0:
                inv = 1.0 / (1.0 + below)
                off = x * inv
            else:
                inv = 1.0 / (1.0 + above * (1.0 - factor) + below)
                off = (x + above * off) * inv
            factor = below * inv
            above = below
            off_all[k, v:v + 2, :] = off
            fac[k, v:v + 2, :] = factor
        return off, factor, below

    off, factor, below = eliminate(0, 0, True)
    code = (local + 1).astype(F32)
    blank = jnp.zeros_like(code)
    even = jnp.concatenate([off[0:1], factor[0:1], code, blank], axis=0)
    odd = jnp.concatenate([off[1:2], below[1:2], code, blank], axis=0)
    wide = jnp.concatenate([
        jnp.concatenate(halves(even), axis=0), jnp.concatenate(halves(odd), axis=0)], axis=1)
    owner8 = jnp.broadcast_to(owner, (8, cols))

    def dispatch(g, c):
        for t in range(GROUP // 2):
            parts = []
            for u in range(2):
                m = owner8 == g * GROUP + 2 * t + u
                parts.append(jnp.where(jnp.concatenate([m, m], axis=1), wide, 0.0))
            lhs[pl.ds(16 * t, 16), :] = jnp.concatenate(parts, axis=0).astype(BF16)
        out = dot(lhs[...], rout[0:LANES, :], NT)
        for d in range(GROUP):
            send1[g * GROUP + d] = out[8 * d:8 * d + 4] + out[8 * d + 4:8 * d + 8]
        return c

    each_group(dispatch, 0)
    recv1[me] = send1[me]

    pl.semaphore_wait(barrier, n - 1)

    def send(src, dst, ss, rs):
        def one(o):
            q = peer(o)
            pltpu.make_async_remote_copy(
                src_ref=src.at[q], dst_ref=dst.at[me], send_sem=ss, recv_sem=rs,
                device_id=q, device_id_type=pl.DeviceIdType.LOGICAL).start()
        peers(one)

    def wait_all(buf, sem):
        part = buf.at[pl.ds(0, n - 1)]
        pltpu.make_async_copy(part, part, sem).wait()

    send(send1, recv1, s1, r1)

    eliminate(1, 2, False)
    for c in loads[1:]:
        c.wait()
    present = jnp.concatenate(
        [jnp.ones((1, cols), F32), flag[...].astype(F32)], axis=0)
    share = frac[...] * present
    share = share / jnp.sum(share, axis=0, keepdims=True)

    wait_all(recv1, r1)
    lane = lax.broadcasted_iota(I32, (4, LANES), 1)
    left = lane < HALF
    slots = GROUP * HALF

    def collect(g, acc):
        evens, odds = [], []
        for m in range(GROUP // 2):
            a = recv1[g * GROUP + 2 * m]
            b = recv1[g * GROUP + 2 * m + 1]
            evens.append(jnp.where(left, a, pltpu.roll(b, HALF, 1)))
            odds.append(jnp.where(left, pltpu.roll(a, HALF, 1), b))
        even = jnp.concatenate(evens, axis=1)
        odd = jnp.concatenate(odds, axis=1)
        at = even[2:3].astype(I32) - 1
        high, low = halves(jnp.concatenate([even[0:2], odd[0:2]], axis=0))
        v = jnp.concatenate([high, low], axis=0)
        at8 = jnp.broadcast_to(at, (8, slots))
        far = at8 // LANES
        far = jnp.where(at8 < 0, -1, far)
        code_h[g] = far
        within = at - far[0:1] * LANES
        jl = one_hot(lax.broadcasted_iota(I32, (LANES, slots), 0) == within)
        near[g] = jl
        rows = jnp.concatenate(
            [jnp.where(far == h, v, 0.0) for h in range(blocks)], axis=0).astype(BF16)
        return acc + dot(rows, jl, NT)

    got = each_group(collect, jnp.zeros((8 * blocks, LANES), F32))
    x = jnp.concatenate(
        [got[8 * h:8 * h + 4] + got[8 * h + 4:8 * h + 8] for h in range(blocks)], axis=1)
    kinds = base.shape[0]
    off_h, fac_s, off_m, exch = [jnp.broadcast_to(x[i:i + 1], (kinds, cols)) for i in range(4)]
    bottom = base[...]
    absorbed = flux[...]
    coupled = link[...]
    temp = bottom
    for _ in range(SWEEPS):
        sat = 0.6 * jnp.exp(0.3 * temp)
        mean_heat = jnp.sum(share * temp, axis=0, keepdims=True)
        mean_moist = jnp.sum(share * sat, axis=0, keepdims=True)
        air_heat = off_h + fac_s * mean_heat
        air_moist = off_m + fac_s * mean_moist
        emitted = 0.5 * jnp.exp(0.2 * temp)
        imbalance = (absorbed - emitted - exch * (temp - air_heat)
                     - 2.5 * exch * (sat - air_moist) - coupled * (temp - bottom))
        slope = 0.2 * emitted + exch * (1.0 + 2.5 * 0.3 * sat) + coupled
        temp = temp + imbalance / slope
    kelvin[...] = temp
    sat = 0.6 * jnp.exp(0.3 * temp)
    mean_heat = jnp.sum(share * temp, axis=0, keepdims=True)
    mean_moist = jnp.sum(share * sat, axis=0, keepdims=True)
    reply = jnp.concatenate([mean_heat, mean_moist, drift[...]], axis=0)
    reply = jnp.concatenate(halves(reply), axis=0)
    reply = jnp.concatenate(
        [reply[:, h * LANES:(h + 1) * LANES] for h in range(blocks)], axis=0).astype(BF16)
    left2 = lax.broadcasted_iota(I32, (2, LANES), 1) < HALF

    def answer(g, c):
        raw = dot(reply, near[g], NN)
        far = code_h[g]
        y = jnp.zeros((8, slots), F32)
        for h in range(blocks):
            y = y + jnp.where(far == h, raw[8 * h:8 * h + 8], 0.0)
        y = y[0:4] + y[4:8]
        for m in range(GROUP // 2):
            tile = y[:, m * LANES:(m + 1) * LANES]
            turned = pltpu.roll(tile, HALF, 1)
            send2[g * GROUP + 2 * m] = jnp.where(left2, tile[0:2], turned[2:4])
            send2[g * GROUP + 2 * m + 1] = jnp.where(left2, turned[0:2], tile[2:4])
        return c

    each_group(answer, 0)
    recv2[me] = send2[me]
    send(send2, recv2, s2, r2)
    wait_all(recv2, r2)

    row = lax.broadcasted_iota(I32, (8, cols), 0) // 2
    shifted = owner8 - row

    def gather(g, acc):
        r = jnp.concatenate([recv2[g * GROUP + d] for d in range(GROUP)], axis=0)
        high, low = halves(r)
        both = jnp.concatenate([high, low], axis=1).astype(BF16)
        raw = dot(both, rout[...], NN)
        for t in range(GROUP // 4):
            m = shifted == g * GROUP + 4 * t
            acc = acc + jnp.where(jnp.concatenate([m, m], axis=1), raw[8 * t:8 * t + 8], 0.0)
        return acc

    acc = each_group(gather, jnp.zeros((8, 2 * cols), F32))
    acc = acc[0:4] + acc[4:8]
    acc = acc[0:2] + acc[2:4]
    boundary[...] = jnp.concatenate([acc[:, :cols], acc[:, cols:]], axis=0)
    wait_all(send1, s1)
    wait_all(send2, s2)


def finish(pieces, off, fac, boundary, kelvin, adv_hbm, kelvin_hbm, adv, out_sem, kelvin_sem):
    levels = off.shape[0]
    step = levels // pieces
    kelvin_out = pltpu.make_async_copy(kelvin, kelvin_hbm, kelvin_sem)
    kelvin_out.start()
    value = boundary[...]
    outs = []
    for k in reversed(range(levels)):
        value = off[k] + fac[k] * value
        adv[k] = value
        if k % step == 0:
            rows = pl.ds(k, step)
            outs.append(pltpu.make_async_copy(
                adv.at[rows], adv_hbm.at[rows], out_sem.at[k // step]))
            outs[-1].start()
    kelvin_out.wait()
    for c in outs:
        c.wait()


def per_device(sizes, *args):
    gx, gy, sa = sizes
    n = gx * gy * sa
    levels, fields, cols = args[0].shape
    kinds = args[7].shape[0]
    assert n % GROUP == 0 and 2 * cols // n <= HALF and cols % LANES == 0
    groups = n // GROUP
    pieces = 4 if levels % 4 == 0 else 1
    vmem = [pltpu.VMEM(a.shape, a.dtype) for a in args]
    off, fac, boundary, kelvin = pl.pallas_call(
        functools.partial(kernel, (gx, gy, sa, levels, cols, pieces)),
        out_shape=(
            pltpu.VMEM(args[0].shape, F32),
            pltpu.VMEM(args[0].shape, F32),
            pltpu.VMEM((fields, cols), F32),
            pltpu.VMEM((kinds, cols), F32),
        ),
        in_specs=[pl.BlockSpec(memory_space=pltpu.HBM)] * len(args),
        out_specs=[pl.BlockSpec(memory_space=pltpu.VMEM)] * 4,
        scratch_shapes=vmem + [
            pltpu.VMEM((2 * LANES, 2 * cols), BF16),
            pltpu.VMEM((8 * GROUP, 2 * cols), BF16),
            pltpu.VMEM((groups, LANES, GROUP * HALF), BF16),
            pltpu.VMEM((groups, 8, GROUP * HALF), I32),
            pltpu.VMEM((n, 4, LANES), F32),
            pltpu.VMEM((n, 4, LANES), F32),
            pltpu.VMEM((n, 2, LANES), F32),
            pltpu.VMEM((n, 2, LANES), F32),
            pltpu.SemaphoreType.DMA((7,)),
            pltpu.SemaphoreType.DMA((2, pieces)),
            pltpu.SemaphoreType.DMA,
            pltpu.SemaphoreType.DMA,
            pltpu.SemaphoreType.DMA,
            pltpu.SemaphoreType.DMA,
        ],
        compiler_params=pltpu.CompilerParams(
            collective_id=0, has_side_effects=True, vmem_limit_bytes=VMEM_GRANT),
    )(*args)
    return pl.pallas_call(
        functools.partial(finish, pieces),
        out_shape=(
            jax.ShapeDtypeStruct(args[0].shape, F32),
            jax.ShapeDtypeStruct((kinds, cols), F32),
        ),
        in_specs=[pl.BlockSpec(memory_space=pltpu.VMEM)] * 4,
        out_specs=[pl.BlockSpec(memory_space=pltpu.HBM)] * 2,
        scratch_shapes=[
            pltpu.VMEM(args[0].shape, F32),
            pltpu.SemaphoreType.DMA((pieces,)),
            pltpu.SemaphoreType.DMA,
        ],
        compiler_params=pltpu.CompilerParams(vmem_limit_bytes=FINISH_GRANT),
    )(off, fac, boundary, kelvin)


def solution(mesh):
    wide = P(None, None, AXES)
    flat = P(None, AXES)
    return jax.shard_map(
        functools.partial(per_device, tuple(mesh.shape[a] for a in AXES)),
        mesh=mesh,
        in_specs=(wide, wide) + (flat,) * 7,
        out_specs=(wide, flat),
        check_vma=False,
    )
```

profile of v0, /device:TPU:0, one launch (start us, length us, event | category | flops | bytes accessed | tf_op | source)
XLA Modules:
  0.0 19.3 jit_solution(5650929256604900504)
XLA Ops:
  0.6 17.8 %shard_map.104 = (f32[32,4,1024]{2,1,0:T(4,128)S(1)}, f32[32,4,1024]{2,1,0:T(4,128)S(1)}, f32[4,1024]{1,0:T(4,128)S(1)}, f32[6,1024]{1,0:T(8,128)S(1)}) custom-call(f32[32,4,1024]{2,1,0:T(4,128)} %prof_hbm.1, f32[32,2,1024]{2,1,0:T(2,128)} %turb_hbm.1, s32[2,1024]{1,0:T(2,128)} %owner_hbm.1, f32[6,1024]{1,0:T(8,128)} %frac_hbm.1, s32[5,1024]{1,0:T(8,128)} %flag_hbm.1, ...), custom_call_target="tpu_custom_call" | custom-call | tf_op jit(solution)/shard_map/pallas_call | solution.py:312
  18.4 0.8 %shard_map.105 = (f32[32,4,1024]{2,1,0:T(4,128)}, f32[6,1024]{1,0:T(8,128)}) custom-call(f32[32,4,1024]{2,1,0:T(4,128)S(1)} %get-tuple-element.6.off, f32[32,4,1024]{2,1,0:T(4,128)S(1)} %get-tuple-element.7.fac, f32[4,1024]{1,0:T(4,128)S(1)} %get-tuple-element.8.boundary, f32[6,1024]{1,0:T(8,128)S(1)} %get-tuple-element.9.kelvin), custom_call_target="tpu_custom_call" | custom-call | tf_op jit(solution)/shard_map/pallas_call | solution.py:341
where the time goes:
time: 19.4 us; the launch traced here: 19.3 us
  Pallas kernels  18.6 us (96%)
  between operations  0.64 us (3%)
    pallas_call x1, Pallas kernels, per_device(): pl.pallas_call(functools.partial(kernel, (gx, gy, sa, levels, cols, piece...  17.8 us
    pallas_call x1, Pallas kernels, per_device(): pl.pallas_call(functools.partial(finish, pieces), out_shape=(jax.ShapeDty...  0.85 us

commit v1 on v0

--- a/solution.py
+++ b/solution.py
@@ -47,24 +47,33 @@
     step = levels // pieces
     me = (lax.axis_index("gx") * gy + lax.axis_index("gy")) * sa + lax.axis_index("sa")
 
-    def peer(o):
-        q = me + o
-        return jnp.where(q >= n, q - n, q)
+    mine = lax.axis_index("gx")
+    upper = 2 * mine >= gx
+    crew = n // gx
+
+    def peer(t):
+        q = jnp.where(upper, t, n - 2 - t)
+        return q + jnp.where(q >= me, 1, 0)
 
     def peers(fn):
         if n <= GROUP:
-            for o in range(1, n):
+            for o in range(n - 1):
                 fn(o)
         else:
             def body(o, c):
                 fn(o)
                 return c
-            lax.fori_loop(1, n, body, 0)
-
-    def each_group(fn, init):
-        if groups == 1:
-            return fn(0, init)
-        return lax.fori_loop(0, groups, fn, init)
+            lax.fori_loop(0, n - 1, body, 0)
+
+    def each(count, fn, init):
+        if count > 4:
+            return lax.fori_loop(0, count, fn, init)
+        for i in range(count):
+            init = fn(i, init)
+        return init
+
+    def crew_at(i):
+        return jnp.where(upper, gx - 1 - i, i)
 
     loads = [
         pltpu.make_async_copy(a, b, in_sem.at[i])
@@ -155,8 +164,7 @@
             send1[g * GROUP + d] = out[8 * d:8 * d + 4] + out[8 * d + 4:8 * d + 8]
         return c
 
-    each_group(dispatch, 0)
-    recv1[me] = send1[me]
+    each(groups, dispatch, 0)
 
     pl.semaphore_wait(barrier, n - 1)
 
@@ -172,7 +180,8 @@
         part = buf.at[pl.ds(0, n - 1)]
         pltpu.make_async_copy(part, part, sem).wait()
 
-    send(send1, recv1, s1, r1)
+    send(send1, recv1, s1, r1.at[mine])
+    pltpu.make_async_copy(send1.at[me], recv1.at[me], r1.at[mine]).start()
 
     eliminate(1, 2, False)
     for c in loads[1:]:
@@ -182,16 +191,18 @@
     share = frac[...] * present
     share = share / jnp.sum(share, axis=0, keepdims=True)
 
-    wait_all(recv1, r1)
     lane = lax.broadcasted_iota(I32, (4, LANES), 1)
     left = lane < HALF
-    slots = GROUP * HALF
-
-    def collect(g, acc):
+    slots = crew * HALF
+
+    def collect(i, acc):
+        first = crew_at(i) * crew
+        part = recv1.at[pl.ds(first, crew)]
+        pltpu.make_async_copy(part, part, r1.at[crew_at(i)]).wait()
         evens, odds = [], []
-        for m in range(GROUP // 2):
-            a = recv1[g * GROUP + 2 * m]
-            b = recv1[g * GROUP + 2 * m + 1]
+        for m in range(crew // 2):
+            a = recv1[first + 2 * m]
+            b = recv1[first + 2 * m + 1]
             evens.append(jnp.where(left, a, pltpu.roll(b, HALF, 1)))
             odds.append(jnp.where(left, pltpu.roll(a, HALF, 1), b))
         even = jnp.concatenate(evens, axis=1)
@@ -202,15 +213,15 @@
         at8 = jnp.broadcast_to(at, (8, slots))
         far = at8 // LANES
         far = jnp.where(at8 < 0, -1, far)
-        code_h[g] = far
+        code_h[i] = far
         within = at - far[0:1] * LANES
         jl = one_hot(lax.broadcasted_iota(I32, (LANES, slots), 0) == within)
-        near[g] = jl
+        near[i] = jl
         rows = jnp.concatenate(
             [jnp.where(far == h, v, 0.0) for h in range(blocks)], axis=0).astype(BF16)
         return acc + dot(rows, jl, NT)
 
-    got = each_group(collect, jnp.zeros((8 * blocks, LANES), F32))
+    got = each(gx, collect, jnp.zeros((8 * blocks, LANES), F32))
     x = jnp.concatenate(
         [got[8 * h:8 * h + 4] + got[8 * h + 4:8 * h + 8] for h in range(blocks)], axis=1)
     kinds = base.shape[0]
@@ -240,21 +251,22 @@
         [reply[:, h * LANES:(h + 1) * LANES] for h in range(blocks)], axis=0).astype(BF16)
     left2 = lax.broadcasted_iota(I32, (2, LANES), 1) < HALF
 
-    def answer(g, c):
-        raw = dot(reply, near[g], NN)
-        far = code_h[g]
+    def answer(i, c):
+        first = crew_at(i) * crew
+        raw = dot(reply, near[i], NN)
+        far = code_h[i]
         y = jnp.zeros((8, slots), F32)
         for h in range(blocks):
             y = y + jnp.where(far == h, raw[8 * h:8 * h + 8], 0.0)
         y = y[0:4] + y[4:8]
-        for m in range(GROUP // 2):
+        for m in range(crew // 2):
             tile = y[:, m * LANES:(m + 1) * LANES]
             turned = pltpu.roll(tile, HALF, 1)
-            send2[g * GROUP + 2 * m] = jnp.where(left2, tile[0:2], turned[2:4])
-            send2[g * GROUP + 2 * m + 1] = jnp.where(left2, turned[0:2], tile[2:4])
+            send2[first + 2 * m] = jnp.where(left2, tile[0:2], turned[2:4])
+            send2[first + 2 * m + 1] = jnp.where(left2, turned[0:2], tile[2:4])
         return c
 
-    each_group(answer, 0)
+    each(gx, answer, 0)
     recv2[me] = send2[me]
     send(send2, recv2, s2, r2)
     wait_all(recv2, r2)
@@ -272,7 +284,7 @@
             acc = acc + jnp.where(jnp.concatenate([m, m], axis=1), raw[8 * t:8 * t + 8], 0.0)
         return acc
 
-    acc = each_group(gather, jnp.zeros((8, 2 * cols), F32))
+    acc = each(groups, gather, jnp.zeros((8, 2 * cols), F32))
     acc = acc[0:4] + acc[4:8]
     acc = acc[0:2] + acc[2:4]
     boundary[...] = jnp.concatenate([acc[:, :cols], acc[:, cols:]], axis=0)
@@ -322,8 +334,8 @@
         scratch_shapes=vmem + [
             pltpu.VMEM((2 * LANES, 2 * cols), BF16),
             pltpu.VMEM((8 * GROUP, 2 * cols), BF16),
-            pltpu.VMEM((groups, LANES, GROUP * HALF), BF16),
-            pltpu.VMEM((groups, 8, GROUP * HALF), I32),
+            pltpu.VMEM((gx, LANES, n // gx * HALF), BF16),
+            pltpu.VMEM((gx, 8, n // gx * HALF), I32),
             pltpu.VMEM((n, 4, LANES), F32),
             pltpu.VMEM((n, 4, LANES), F32),
             pltpu.VMEM((n, 2, LANES), F32),
@@ -331,7 +343,7 @@
             pltpu.SemaphoreType.DMA((7,)),
             pltpu.SemaphoreType.DMA((2, pieces)),
             pltpu.SemaphoreType.DMA,
-            pltpu.SemaphoreType.DMA,
+            pltpu.SemaphoreType.DMA((gx,)),
             pltpu.SemaphoreType.DMA,
             pltpu.SemaphoreType.DMA,
         ],

time: 19.4 us -> 18.7 us (0.964)
  Pallas kernels: 18.6 us -> 17.9 us
    pallas_call x1, Pallas kernels: 17.8 us -> 17.1 us  [per_device(): pl.pallas_call(functools.partial(kernel, (gx, gy, sa, levels, cols, piece...]
where the time goes in v1:
time: 18.7 us; the launch traced here: 18.6 us
  Pallas kernels  17.9 us (96%)
  between operations  0.64 us (3%)
    pallas_call x1, Pallas kernels, per_device(): pl.pallas_call(functools.partial(kernel, (gx, gy, sa, levels, cols, piece...  17.1 us
    pallas_call x1, Pallas kernels, per_device(): pl.pallas_call(functools.partial(finish, pieces), out_shape=(jax.ShapeDty...  0.85 us

profile of v1, /device:TPU:0, one launch (start us, length us, event | category | flops | bytes accessed | tf_op | source)
XLA Modules:
  0.0 18.6 jit_solution(11152826726027965653)
XLA Ops:
  0.6 17.1 %shard_map.104 = (f32[32,4,1024]{2,1,0:T(4,128)S(1)}, f32[32,4,1024]{2,1,0:T(4,128)S(1)}, f32[4,1024]{1,0:T(4,128)S(1)}, f32[6,1024]{1,0:T(8,128)S(1)}) custom-call(f32[32,4,1024]{2,1,0:T(4,128)} %prof_hbm.1, f32[32,2,1024]{2,1,0:T(2,128)} %turb_hbm.1, s32[2,1024]{1,0:T(2,128)} %owner_hbm.1, f32[6,1024]{1,0:T(8,128)} %frac_hbm.1, s32[5,1024]{1,0:T(8,128)} %flag_hbm.1, ...), custom_call_target="tpu_custom_call" | custom-call | tf_op jit(solution)/shard_map/pallas_call | solution.py:324
  17.7 0.8 %shard_map.105 = (f32[32,4,1024]{2,1,0:T(4,128)}, f32[6,1024]{1,0:T(8,128)}) custom-call(f32[32,4,1024]{2,1,0:T(4,128)S(1)} %get-tuple-element.6.off, f32[32,4,1024]{2,1,0:T(4,128)S(1)} %get-tuple-element.7.fac, f32[4,1024]{1,0:T(4,128)S(1)} %get-tuple-element.8.boundary, f32[6,1024]{1,0:T(8,128)S(1)} %get-tuple-element.9.kelvin), custom_call_target="tpu_custom_call" | custom-call | tf_op jit(solution)/shard_map/pallas_call | solution.py:353

commit v2 on v1

--- a/solution.py
+++ b/solution.py
@@ -55,15 +55,15 @@
         q = jnp.where(upper, t, n - 2 - t)
         return q + jnp.where(q >= me, 1, 0)
 
-    def peers(fn):
+    def peers(fn, start=0, count=n - 1):
         if n <= GROUP:
-            for o in range(n - 1):
-                fn(o)
+            for o in range(count):
+                fn(start + o)
         else:
             def body(o, c):
                 fn(o)
                 return c
-            lax.fori_loop(0, n - 1, body, 0)
+            lax.fori_loop(start, start + count, body, 0)
 
     def each(count, fn, init):
         if count > 4:
@@ -168,13 +168,13 @@
 
     pl.semaphore_wait(barrier, n - 1)
 
-    def send(src, dst, ss, rs):
+    def send(src, dst, ss, rs, start=0, count=n - 1):
         def one(o):
             q = peer(o)
             pltpu.make_async_remote_copy(
                 src_ref=src.at[q], dst_ref=dst.at[me], send_sem=ss, recv_sem=rs,
                 device_id=q, device_id_type=pl.DeviceIdType.LOGICAL).start()
-        peers(one)
+        peers(one, start, count)
 
     def wait_all(buf, sem):
         part = buf.at[pl.ds(0, n - 1)]
@@ -266,9 +266,16 @@
             send2[first + 2 * m + 1] = jnp.where(left2, turned[0:2], tile[2:4])
         return c
 
-    each(gx, answer, 0)
+    def answer_far(c, carry):
+        answer(gx - 1 - c, 0)
+        send(send2, recv2, s2, r2, c * crew, crew)
+        return carry
+
+    far_planes = gx // 2
+    each(far_planes, answer_far, 0)
+    each(gx - far_planes, answer, 0)
     recv2[me] = send2[me]
-    send(send2, recv2, s2, r2)
+    send(send2, recv2, s2, r2, far_planes * crew, n - 1 - far_planes * crew)
     wait_all(recv2, r2)
 
     row = lax.broadcasted_iota(I32, (8, cols), 0) // 2

time: 18.7 us -> 18.6 us (level)
  no operation moved by 1% of the time
where the time goes in v2:
time: 18.6 us; the launch traced here: 18.5 us
  Pallas kernels  17.8 us (96%)
  between operations  0.64 us (3%)
    pallas_call x1, Pallas kernels, per_device(): pl.pallas_call(functools.partial(kernel, (gx, gy, sa, levels, cols, piece...  17 us
    pallas_call x1, Pallas kernels, per_device(): pl.pallas_call(functools.partial(finish, pieces), out_shape=(jax.ShapeDty...  0.85 us

profile of v2, /device:TPU:0, one launch (start us, length us, event | category | flops | bytes accessed | tf_op | source)
XLA Modules:
  0.0 18.5 jit_solution(7562761899500568345)
XLA Ops:
  0.6 17.0 %shard_map.104 = (f32[32,4,1024]{2,1,0:T(4,128)S(1)}, f32[32,4,1024]{2,1,0:T(4,128)S(1)}, f32[4,1024]{1,0:T(4,128)S(1)}, f32[6,1024]{1,0:T(8,128)S(1)}) custom-call(f32[32,4,1024]{2,1,0:T(4,128)} %prof_hbm.1, f32[32,2,1024]{2,1,0:T(2,128)} %turb_hbm.1, s32[2,1024]{1,0:T(2,128)} %owner_hbm.1, f32[6,1024]{1,0:T(8,128)} %frac_hbm.1, s32[5,1024]{1,0:T(8,128)} %flag_hbm.1, ...), custom_call_target="tpu_custom_call" | custom-call | tf_op jit(solution)/shard_map/pallas_call | solution.py:331
  17.6 0.8 %shard_map.105 = (f32[32,4,1024]{2,1,0:T(4,128)}, f32[6,1024]{1,0:T(8,128)}) custom-call(f32[32,4,1024]{2,1,0:T(4,128)S(1)} %get-tuple-element.6.off, f32[32,4,1024]{2,1,0:T(4,128)S(1)} %get-tuple-element.7.fac, f32[4,1024]{1,0:T(4,128)S(1)} %get-tuple-element.8.boundary, f32[6,1024]{1,0:T(8,128)S(1)} %get-tuple-element.9.kelvin), custom_call_target="tpu_custom_call" | custom-call | tf_op jit(solution)/shard_map/pallas_call | solution.py:360
